TPU v7x, 32 devices: a whole 2x2x4 slice. The times are simulated.
32 devices in a mesh: harm: 8 (over y, x, core), mode: 4 (over z).
Axes of the slice: x: 2, y: 2, z: 4, core: 2. Of those that a mesh axis runs over, the one named last changes fastest.
Arguments:
- mode_vectors: float32 [49152, 1024], P('harm', 'mode'), may hold values from -0.09375 to 0.09375
- weights: float32 [49152, 1024], P('harm', 'mode'), may hold values from -0.1875 to 0.1875
- cotangent: float32 [49152, 1024], P('harm', 'mode'), may hold values from -6 to 6
- eigenvalues: float32 [1024], replicated, may hold values from 0 to 4
- eigen_cotangent: float32 [1024], replicated, may hold values from -6 to 6
- slab_rows: int32 [4096], replicated, may hold values from 0 to 49151, as said below
Outputs:
- slab: float32 [4096, 49152], P('mode', 'harm')
Inputs may be any that keep to these rules, and one draw needn't show every extreme that they name: `slab_rows`: each block of 6144 consecutive harmonics (0 to 6143, 6144 to 12287 and so on) holds exactly 512 of the slab rows.
All inputs are finite; a program needn't handle non-finite values.
Results may differ from a plain program's by a relative error of at most 0.0001.
Values sent between devices are 32-bit elements; how exact they have to be, the bound alone decides.
A program may use at most 128 MiB of HBM per device.

v0:
```python
import jax
import jax.numpy as jnp
from jax import lax
from jax.sharding import PartitionSpec as P

regular = 0.01
precision = lax.Precision.HIGHEST


def product(left, right, left_dim, right_dim):
    return lax.dot_general(
        left,
        right,
        (((left_dim,), (right_dim,)), ((), ())),
        precision=precision,
        preferred_element_type=jnp.float32,
    )


def weigh_gap(block, row_ids, col_ids, eigenvalues, eigen_cotangent):
    eigen_rows = lax.dynamic_slice_in_dim(eigenvalues, row_ids, block.shape[0])
    eigen_cols = lax.dynamic_slice_in_dim(eigenvalues, col_ids, block.shape[1])
    slope_cols = lax.dynamic_slice_in_dim(eigen_cotangent, col_ids, block.shape[1])
    differ = eigen_cols[None, :] - eigen_rows[:, None]
    factor = differ / (differ * differ + regular)
    rows = row_ids + lax.broadcasted_iota(jnp.int32, block.shape, 0)
    cols = col_ids + lax.broadcasted_iota(jnp.int32, block.shape, 1)
    return factor * block + jnp.where(rows == cols, slope_cols[None, :], 0.0)


def pick_rows(table, slab_rows, harm_index):
    row_count = table.shape[0]
    offset = slab_rows - harm_index * row_count
    inside = (offset >= 0) & (offset < row_count)
    picked = jnp.take(table, jnp.clip(offset, 0, row_count - 1), axis=0)
    return jnp.where(inside[:, None], picked, 0.0)


def gather_weights(weights, slab_rows, harm_index, harm_count, mode_count):
    width = weights.shape[1]
    with jax.named_scope("pick"):
        picked = pick_rows(weights, slab_rows, harm_index)
    piece = slab_rows.shape[0] // (harm_count * mode_count)
    picked = picked.reshape(mode_count, harm_count, piece, width)
    with jax.named_scope("sum_weights"):
        picked = lax.psum_scatter(picked, "harm", scatter_dimension=1, tiled=True)
    picked = picked.reshape(mode_count, piece, width)
    with jax.named_scope("swap"):
        swapped = lax.all_to_all(picked, "mode", split_axis=0, concat_axis=2, tiled=True)
    with jax.named_scope("spread_weights"):
        return lax.all_gather(
            swapped.reshape(piece, mode_count * width), "harm", axis=0, tiled=True
        )


def plain(
    mode_vectors,
    weights,
    cotangent,
    eigenvalues,
    eigen_cotangent,
    slab_rows,
    harm_count,
    mode_count,
):
    harm_index = lax.axis_index("harm")
    width = mode_vectors.shape[1]
    modes = width * mode_count
    full = lax.all_gather(mode_vectors, "mode", axis=1, tiled=True)
    owned_weights = gather_weights(weights, slab_rows, harm_index, harm_count, mode_count)
    gram = product(full, cotangent, 0, 0)
    gram = lax.psum_scatter(gram, "harm", scatter_dimension=0, tiled=True)
    weighted = weigh_gap(
        gram,
        harm_index * (modes // harm_count),
        lax.axis_index("mode") * width,
        eigenvalues,
        eigen_cotangent,
    )
    weighted = lax.all_gather(weighted, "mode", axis=1, tiled=True)
    weighted = lax.all_gather(weighted, "harm", axis=0, tiled=True)
    return product(product(owned_weights, weighted, 1, 0), full, 1, 1)


def solution(mesh):
    harm_count = mesh.shape["harm"]
    mode_count = mesh.shape["mode"]
    placed = (P("harm", "mode"), P("harm", "mode"), P("harm", "mode"), P(), P(), P())

    def local(*operands):
        return plain(*operands, harm_count, mode_count)

    return jax.shard_map(
        local, mesh=mesh, in_specs=placed, out_specs=P("mode", "harm"), check_vma=False
    )
```

profile of v0, /device:TPU:0, one launch (start us, length us, event | category | flops | bytes accessed | tf_op | source)
XLA Modules:
  0.0 702.6 jit_solution(5876162007898497041)
XLA Ops:
  7.4 0.0 copy-start
  7.4 0.0 all-gather.6.cloned.1.call-start
  7.4 0.7 all-gather.6.cloned.1.call-update
  8.1 0.0 reduce-scatter.3.cloned.1.call-start
  8.1 0.0 copy-done
  8.2 18.9 %gather_fusion = f32[4096,256]{1,0:T(8,128)} fusion(f32[6144,256]{1,0:T(8,128)} %param.7, s32[4096]{0:T(1024)S(1)} %fusion.3), kind=kCustom, calls=%fused_computation | custom fusion | bytes 8404992 | tf_op jit(solution)/shard_map/pick/jit(_take)/gather | solution.py:35
  27.2 5.6 copy.10
  32.7 5.5 select_select_fusion
  38.3 0.0 reduce-scatter.3.cloned.1.call-update
  38.3 0.0 reduce-scatter.5.cloned.1.call-start
  38.3 399.3 %all-gather.6.cloned.1.call-done = f32[6144,1024]{1,0:T(8,128)} async-done(((f32[6144,256]{1,0:T(8,128)}), f32[6144,1024]{1,0:T(8,128)}) %all-gather.6.cloned.1.call-update) | async-done | bytes 25165840 | tf_op jit(solution)/shard_map/all_gather | solution.py:69
  437.7 44.0 %fusion.4 = f32[1024,256]{1,0:T(8,128)} fusion(f32[6144,1024]{1,0:T(8,128)} %all-gather.6.cloned.1.call-done, f32[6144,256]{1,0:T(8,128)} %param.8), kind=kOutput, calls=%fused_computation.13 | convolution fusion | flops 19327352832 | bytes 32505856 | tf_op jit(solution)/shard_map/dot_general | solution.py:11
  481.6 0.0 reduce-scatter.5.cloned.1.call-update
  481.6 0.0 all-gather.4.cloned.1.call-start
  481.7 0.0 reduce-scatter.3.cloned.1.call-done
  481.7 19.2 %all_to_all.15 = f32[4,128,256]{1,2,0:T(8,128)} all-to-all(f32[4,128,256]{1,2,0:T(8,128)} %bitcast.19), channel_id=1, replica_groups=mesh['harm'=8,'mode'=4] {'mode'}, dimensions={0} | all-to-all | bytes 1048576 | tf_op jit(solution)/shard_map/swap/all_to_all | solution.py:49
  500.9 0.0 all-gather.4.cloned.1.call-update
  500.9 0.0 all-gather.8.cloned.1.call-start
  501.0 0.8 dynamic_slice.10
  501.7 0.8 dynamic_slice.9
  502.5 0.8 dynamic_slice.11
  503.2 12.6 %reduce-scatter.5.cloned.1.call-done = f32[128,256]{1,0:T(8,128)} async-done(((f32[1024,256]{1,0:T(8,128)}), f32[128,256]{1,0:T(8,128)}) %reduce-scatter.5.cloned.1.call-update) | async-done | bytes 131088 | tf_op jit(solution)/shard_map/reduce_scatter | solution.py:72
  515.8 1.0 fusion.2
  516.9 15.9 %all_gather.14 = f32[128,1024]{1,0:T(8,128)} all-gather(f32[128,256]{1,0:T(8,128)S(1)} %fusion.2), channel_id=1, replica_groups=mesh['harm'=8,'mode'=4] {'mode'}, dimensions={1}, use_global_device_ids=true | all-gather | bytes 655360 | tf_op jit(solution)/shard_map/all_gather | solution.py:80
  532.8 0.0 all-gather.8.cloned.1.call-update
  532.8 22.0 %all-gather.4.cloned.1.call-done = f32[1024,1024]{0,1:T(8,128)} async-done(((f32[128,1024]{0,1:T(8,128)}), f32[1024,1024]{0,1:T(8,128)}) %all-gather.4.cloned.1.call-update) | async-done | bytes 4194320 | tf_op jit(solution)/shard_map/spread_weights/all_gather | solution.py:51
  554.8 38.4 %all-gather.8.cloned.1.call-done = f32[1024,1024]{1,0:T(8,128)} async-done(((f32[128,1024]{1,0:T(8,128)}), f32[1024,1024]{1,0:T(8,128)}) %all-gather.8.cloned.1.call-update) | async-done | bytes 4194320 | tf_op jit(solution)/shard_map/all_gather | solution.py:81
  593.2 16.6 %fusion.5 = f32[1024,1024]{1,0:T(8,128)S(1)} fusion(f32[1024,1024]{0,1:T(8,128)} %all-gather.4.cloned.1.call-done, f32[1024,1024]{1,0:T(8,128)} %all-gather.8.cloned.1.call-done), kind=kOutput, calls=%fused_computation.14 | convolution fusion | flops 12884901888 | bytes 12582912 | tf_op jit(solution)/shard_map/dot_general | solution.py:11
  609.8 85.2 %fusion.6 = f32[1024,6144]{1,0:T(8,128)} fusion(f32[1024,1024]{1,0:T(8,128)S(1)} %fusion.5, f32[6144,1024]{1,0:T(8,128)} %all-gather.6.cloned.1.call-done), kind=kOutput, calls=%fused_computation.15 | convolution fusion | flops 77309411328 | bytes 54525952 | tf_op jit(solution)/shard_map/dot_general | solution.py:11
  (6 shorter events, 0.1 us)
Async XLA Ops:
  7.4 0.8 copy-start
  7.4 430.3 %all-gather.6.cloned.1.call-start = ((), (), s32[]{:S(2)}) async-start(), calls=%async_computation.5 | async-start | bytes 31457280 | tf_op jit(solution)/shard_map/all_gather | solution.py:69
  8.1 473.6 %reduce-scatter.3.cloned.1.call-start = ((), (), s32[]{:S(2)}) async-start(), calls=%async_computation.3 | async-start | bytes 4718592 | tf_op jit(solution)/shard_map/sum_weights/reduce_scatter | solution.py:46
  38.3 477.6 %reduce-scatter.5.cloned.1.call-start = ((), (), s32[]{:S(2)}) async-start(), calls=%async_computation.6 | async-start | bytes 1179648 | tf_op jit(solution)/shard_map/reduce_scatter | solution.py:72
  481.6 73.2 %all-gather.4.cloned.1.call-start = ((), (), s32[]{:S(2)}) async-start(), calls=%async_computation.4 | async-start | bytes 4718592 | tf_op jit(solution)/shard_map/spread_weights/all_gather | solution.py:51
  500.9 92.3 %all-gather.8.cloned.1.call-start = ((), (), s32[]{:S(2)}) async-start(), calls=%async_computation.7 | async-start | bytes 4718592 | tf_op jit(solution)/shard_map/all_gather | solution.py:81
Sparse Core Ops, SparseCore 0:
  9.7 427.8 all-gather.5
Sparse Core Ops, SparseCore 1:
  38.4 53.7 reduce-scatter.2
  481.7 34.1 reduce-scatter.4
  517.6 37.2 all-gather.3
  556.8 36.4 all-gather.7
where the time goes:
time: 703 us
  waiting for transfers between devices  473 us (67%)
  matrix products  146 us (21%)
  blocking collectives  35.1 us (5%)
  local copies, waits for them, and re-layouts  26.8 us (4%)
  between operations  15.1 us (2%)
    all_gather x1, waiting for transfers between devices, plain(): full = lax.all_gather(mode_vectors, 'mode', axis=1, tiled=True)  399 us
    dot_general x3, matrix products, product(): lax.dot_general(left, right, (((left_dim,), (right_dim,)), ((), ())), pre...  146 us
    all_gather x1, waiting for transfers between devices, plain(): weighted = lax.all_gather(weighted, 'harm', axis=0, tiled=True)  38.4 us
    gather x2, local copies, waits for them, and re-layouts, pick_rows(): picked = jnp.take(table, jnp.clip(offset, 0, row_count - 1), axis=0)  24.5 us
    all_gather x1, waiting for transfers between devices, gather_weights(): lax.all_gather(swapped.reshape(piece, mode_count * width), 'harm', axis=0...  22 us
    all_to_all x1, blocking collectives, gather_weights(): lax.all_to_all(picked, 'mode', split_axis=0, concat_axis=2, tiled=True)  19.2 us
    all_gather x1, blocking collectives, plain(): weighted = lax.all_gather(weighted, 'mode', axis=1, tiled=True)  15.9 us
  transfers between devices with their start and end apart: 5, of which 4 were waited for; matrix products, arithmetic and copies ran while one was open for 11% of the time, Pallas kernels for 0%

commit v1 on v0

--- a/solution.py
+++ b/solution.py
@@ -5,6 +5,36 @@
 
 regular = 0.01
 precision = lax.Precision.HIGHEST
+
+
+def derive_strips_all(vector, row_dim, here_x):
+    t_next, far_arr = (vector.shape[:row_dim], vector.shape[row_dim + 1 :])
+    local_out = vector.reshape(*t_next, here_x, -1, *far_arr)
+    field_out = jnp.moveaxis(local_out, row_dim, 0)
+    return field_out
+
+
+def choose_sums_all(x_part, array_dim):
+    val2 = list(x_part.shape[1:])
+    val2[array_dim] *= x_part.shape[0]
+    state_now = jnp.moveaxis(x_part, 0, array_dim).reshape(val2)
+    return state_now
+
+
+def draft_cycles_for(sheet, a_name, shard_in, block_here):
+    block_next = jax.lax.axis_size(a_name)
+    arr_next = jax.lax.axis_index(a_name)
+    built, near = (block_next, arr_next)
+    fresh = derive_strips_all(sheet, shard_in, built)
+    kept_rows = [fresh[near]]
+    for j in range(1, built):
+        f_next = fresh[near ^ j]
+        q_next = jax.lax.ppermute(f_next, a_name, [(kk, kk ^ j) for kk in range(built)])
+        kept_rows.append(q_next)
+    met_up = jnp.stack(kept_rows, 0)
+    fresh = met_up[near ^ jnp.arange(built)]
+    value_now = choose_sums_all(fresh, block_here)
+    return value_now
 
 
 def product(left, right, left_dim, right_dim):
@@ -46,7 +76,7 @@
         picked = lax.psum_scatter(picked, "harm", scatter_dimension=1, tiled=True)
     picked = picked.reshape(mode_count, piece, width)
     with jax.named_scope("swap"):
-        swapped = lax.all_to_all(picked, "mode", split_axis=0, concat_axis=2, tiled=True)
+        swapped = draft_cycles_for(picked, a_name="mode", shard_in=0, block_here=2)
     with jax.named_scope("spread_weights"):
         return lax.all_gather(
             swapped.reshape(piece, mode_count * width), "harm", axis=0, tiled=True

time: 703 us -> 703 us (level)
  blocking collectives: 35.1 us -> 16.1 us
  waiting for transfers between devices: 473 us -> 490 us
    all_to_all x1 -> x0, blocking collectives: 19.2 us -> none  [gather_weights(): lax.all_to_all(picked, 'mode', split_axis=0, concat_axis=2, tiled=True)]
    ppermute x0 -> x3, waiting for transfers between devices: none -> 7.98 us  [draft_cycles_for(): jax.lax.ppermute(f_next, a_name, [(kk, kk ^ j) for kk in range(built)])]
    gather x2 -> x1, local copies, waits for them, and re-layouts: 24.5 us -> 18.9 us  [pick_rows(): picked = jnp.take(table, jnp.clip(offset, 0, row_count - 1), axis=0)]
  transfers between devices with their start and end apart: 5 -> 8, of which waited for: 4 -> 6; matrix products, arithmetic and copies ran while one was open for 11% -> 11% of each run, Pallas kernels for 0% -> 0%
where the time goes in v1:
time: 703 us
  waiting for transfers between devices  490 us (70%)
  matrix products  146 us (21%)
  local copies, waits for them, and re-layouts  23.9 us (3%)
  blocking collectives  16.1 us (2%)
  between operations  15.2 us (2%)
    all_gather x1, waiting for transfers between devices, plain(): full = lax.all_gather(mode_vectors, 'mode', axis=1, tiled=True)  405 us
    dot_general x3, matrix products, product(): lax.dot_general(left, right, (((left_dim,), (right_dim,)), ((), ())), pre...  146 us
    all_gather x1, waiting for transfers between devices, plain(): weighted = lax.all_gather(weighted, 'harm', axis=0, tiled=True)  38.4 us
    all_gather x1, waiting for transfers between devices, gather_weights(): lax.all_gather(swapped.reshape(piece, mode_count * width), 'harm', axis=0...  21.8 us
    gather x1, local copies, waits for them, and re-layouts, pick_rows(): picked = jnp.take(table, jnp.clip(offset, 0, row_count - 1), axis=0)  18.9 us
    reduce_scatter x1, waiting for transfers between devices, plain(): gram = lax.psum_scatter(gram, 'harm', scatter_dimension=0, tiled=True)  16.5 us
    all_gather x1, blocking collectives, plain(): weighted = lax.all_gather(weighted, 'mode', axis=1, tiled=True)  16.1 us
  transfers between devices with their start and end apart: 8, of which 6 were waited for; matrix products, arithmetic and copies ran while one was open for 11% of the time, Pallas kernels for 0%

profile of v1, /device:TPU:0, one launch (start us, length us, event | category | flops | bytes accessed | tf_op | source)
XLA Modules:
  0.0 702.6 jit_solution(2700233737331766487)
XLA Ops:
  7.4 0.0 copy-start
  7.4 0.0 all-gather.6.cloned.1.call-start
  7.4 0.7 all-gather.6.cloned.1.call-update
  8.1 0.0 reduce-scatter.3.cloned.1.call-start
  8.1 0.0 copy-done
  8.2 18.9 %gather_fusion = f32[4096,256]{1,0:T(8,128)} fusion(f32[6144,256]{1,0:T(8,128)} %param.7, s32[4096]{0:T(1024)S(1)} %fusion.4), kind=kCustom, calls=%fused_computation | custom fusion | bytes 8404992 | tf_op jit(solution)/shard_map/pick/jit(_take)/gather | solution.py:65
  27.2 5.5 fusion
  32.7 0.0 reduce-scatter.3.cloned.1.call-update
  32.7 0.0 reduce-scatter.5.cloned.1.call-start
  32.7 404.9 %all-gather.6.cloned.1.call-done = f32[6144,1024]{1,0:T(8,128)} async-done(((f32[6144,256]{1,0:T(8,128)}), f32[6144,1024]{1,0:T(8,128)}) %all-gather.6.cloned.1.call-update) | async-done | bytes 25165840 | tf_op jit(solution)/shard_map/all_gather | solution.py:99
  437.7 43.9 %fusion.6 = f32[1024,256]{1,0:T(8,128)} fusion(f32[6144,1024]{1,0:T(8,128)} %all-gather.6.cloned.1.call-done, f32[6144,256]{1,0:T(8,128)} %param.8), kind=kOutput, calls=%fused_computation.23 | convolution fusion | flops 19327352832 | bytes 32505856 | tf_op jit(solution)/shard_map/dot_general | solution.py:41
  481.5 0.0 reduce-scatter.5.cloned.1.call-update
  481.6 0.0 all-gather.4.cloned.1.call-start
  481.6 0.0 reduce-scatter.3.cloned.1.call-done
  481.7 1.1 constant_dynamic-slice_fusion
  482.8 0.4 collective-permute-start.2
  483.2 0.4 collective-permute-start.1
  483.6 3.7 collective-permute-start
  487.3 3.9 collective-permute-done.2
  491.2 4.1 collective-permute-done.1
  495.3 0.0 collective-permute-done
  495.3 0.6 gather_fusion.1
  495.9 1.0 copy.12
  496.9 0.0 all-gather.4.cloned.1.call-update
  496.9 0.0 all-gather.8.cloned.1.call-start
  497.0 0.8 dynamic_slice.26
  497.7 0.8 dynamic_slice.25
  498.5 0.8 dynamic_slice.27
  499.3 16.5 %reduce-scatter.5.cloned.1.call-done = f32[128,256]{1,0:T(8,128)} async-done(((f32[1024,256]{1,0:T(8,128)}), f32[128,256]{1,0:T(8,128)}) %reduce-scatter.5.cloned.1.call-update) | async-done | bytes 131088 | tf_op jit(solution)/shard_map/reduce_scatter | solution.py:102
  515.8 1.0 fusion.3
  516.8 16.1 %all_gather.14 = f32[128,1024]{1,0:T(8,128)} all-gather(f32[128,256]{1,0:T(8,128)S(1)} %fusion.3), channel_id=1, replica_groups=mesh['harm'=8,'mode'=4] {'mode'}, dimensions={1}, use_global_device_ids=true | all-gather | bytes 655360 | tf_op jit(solution)/shard_map/all_gather | solution.py:110
  532.9 0.0 all-gather.8.cloned.1.call-update
  532.9 21.8 %all-gather.4.cloned.1.call-done = f32[1024,1024]{0,1:T(8,128)} async-done(((f32[128,1024]{0,1:T(8,128)}), f32[1024,1024]{0,1:T(8,128)}) %all-gather.4.cloned.1.call-update) | async-done | bytes 4194320 | tf_op jit(solution)/shard_map/spread_weights/all_gather | solution.py:81
  554.8 38.4 %all-gather.8.cloned.1.call-done = f32[1024,1024]{1,0:T(8,128)} async-done(((f32[128,1024]{1,0:T(8,128)}), f32[1024,1024]{1,0:T(8,128)}) %all-gather.8.cloned.1.call-update) | async-done | bytes 4194320 | tf_op jit(solution)/shard_map/all_gather | solution.py:111
  593.2 16.6 %fusion.7 = f32[1024,1024]{1,0:T(8,128)S(1)} fusion(f32[1024,1024]{0,1:T(8,128)} %all-gather.4.cloned.1.call-done, f32[1024,1024]{1,0:T(8,128)} %all-gather.8.cloned.1.call-done), kind=kOutput, calls=%fused_computation.24 | convolution fusion | flops 12884901888 | bytes 12582912 | tf_op jit(solution)/shard_map/dot_general | solution.py:41
  609.8 85.2 %fusion.8 = f32[1024,6144]{1,0:T(8,128)} fusion(f32[1024,1024]{1,0:T(8,128)S(1)} %fusion.7, f32[6144,1024]{1,0:T(8,128)} %all-gather.6.cloned.1.call-done), kind=kOutput, calls=%fused_computation.25 | convolution fusion | flops 77309411328 | bytes 54525952 | tf_op jit(solution)/shard_map/dot_general | solution.py:41
  (9 shorter events, 0.1 us)
Async XLA Ops:
  7.4 0.8 copy-start
  7.4 430.3 %all-gather.6.cloned.1.call-start = ((), (), s32[]{:S(2)}) async-start(), calls=%async_computation.4 | async-start | bytes 31457280 | tf_op jit(solution)/shard_map/all_gather | solution.py:99
  8.1 473.6 %reduce-scatter.3.cloned.1.call-start = ((), (), s32[]{:S(2)}) async-start(), calls=%async_computation.2 | async-start | bytes 4718592 | tf_op jit(solution)/shard_map/sum_weights/reduce_scatter | solution.py:76
  32.7 483.1 %reduce-scatter.5.cloned.1.call-start = ((), (), s32[]{:S(2)}) async-start(), calls=%async_computation.5 | async-start | bytes 1179648 | tf_op jit(solution)/shard_map/reduce_scatter | solution.py:102
  481.6 73.2 %all-gather.4.cloned.1.call-start = ((), (), s32[]{:S(2)}) async-start(), calls=%async_computation.3 | async-start | bytes 4718592 | tf_op jit(solution)/shard_map/spread_weights/all_gather | solution.py:81
  482.8 8.4 %collective-permute-start.2 = (f32[1,128,256]{2,1,0:T(8,128)S(1)}, f32[1,128,256]{2,1,0:T(8,128)S(1)}, u32[]{:S(2)}, u32[]{:S(2)}) collective-permute-start(f32[1,128,256]{2,1,0:T(8,128)S(1)} %get-tuple-element.6), channel_id=1, source_target_pairs={{0,3},{1,2},{2,1},{3,0},{4,7},{5,6},{6,5},{7,4},{8,11},{9,10},{10,... | collective-permute-start | bytes 393224 | tf_op jit(solution)/shard_map/swap/ppermute | solution.py:32
  483.2 12.1 %collective-permute-start.1 = (f32[1,128,256]{2,1,0:T(8,128)S(1)}, f32[1,128,256]{2,1,0:T(8,128)S(1)}, u32[]{:S(2)}, u32[]{:S(2)}) collective-permute-start(f32[1,128,256]{2,1,0:T(8,128)S(1)} %get-tuple-element.7), channel_id=1, source_target_pairs={{0,2},{1,3},{2,0},{3,1},{4,6},{5,7},{6,4},{7,5},{8,10},{9,11},{10,... | collective-permute-start | bytes 393224 | tf_op jit(solution)/shard_map/swap/ppermute | solution.py:32
  483.6 11.7 %collective-permute-start = (f32[1,128,256]{2,1,0:T(8,128)S(1)}, f32[1,128,256]{2,1,0:T(8,128)S(1)}, u32[]{:S(2)}, u32[]{:S(2)}) collective-permute-start(f32[1,128,256]{2,1,0:T(8,128)S(1)} %get-tuple-element.8), channel_id=1, source_target_pairs={{0,1},{1,0},{2,3},{3,2},{4,5},{5,4},{6,7},{7,6},{8,9},{9,8},{10,11... | collective-permute-start | bytes 393224 | tf_op jit(solution)/shard_map/swap/ppermute | solution.py:32
  496.9 96.2 %all-gather.8.cloned.1.call-start = ((), (), s32[]{:S(2)}) async-start(), calls=%async_computation.6 | async-start | bytes 4718592 | tf_op jit(solution)/shard_map/all_gather | solution.py:111
Sparse Core Ops, SparseCore 0:
  9.7 427.8 all-gather.5
Sparse Core Ops, SparseCore 1:
  32.8 53.7 reduce-scatter.2
  481.6 34.1 reduce-scatter.4
  517.5 37.2 all-gather.3
  556.7 36.4 all-gather.7
